TPU v7x, 32 devices: a whole 2x2x4 slice. The times are simulated.
32 devices in a mesh: groups: 2 (over y), dap: 4 (over z), chan: 2 (over x), sub: 2 (over core).
Axes of the slice: x: 2, y: 2, z: 4, core: 2. Of those that a mesh axis runs over, the one named last changes fastest.
Arguments:
- pair_input: bfloat16 [768, 384, 128], P(('groups', 'dap'), ('chan', 'sub')), parts along dimension 0, may hold values from -6 to 6
- first_gain: float32 [128], replicated, may hold values from 0.25 to 1.75
- first_project: bfloat16 [128, 512], replicated, may hold values from -0.5 to 0.5
- first_gate: bfloat16 [128, 128], replicated, may hold values from -0.5 to 0.5
- first_norm: float32 [128], replicated, may hold values from 0.25 to 1.75
- first_final: bfloat16 [128, 128], replicated, may hold values from -0.5 to 0.5
- second_gain: float32 [128], replicated, may hold values from 0.25 to 1.75
- second_project: bfloat16 [128, 512], replicated, may hold values from -0.5 to 0.5
- second_gate: bfloat16 [128, 128], replicated, may hold values from -0.5 to 0.5
- second_norm: float32 [128], replicated, may hold values from 0.25 to 1.75
- second_final: bfloat16 [128, 128], replicated, may hold values from -0.5 to 0.5
Outputs:
- pair_output: bfloat16 [768, 384, 128], P(('groups', 'dap'), ('chan', 'sub')), parts along dimension 0
There are 2 independent parts, one for each index of `groups`. A program takes and returns all parts, laid end to end along the dimension named above; an argument that names none is the same for every part. Nothing has to cross between parts.
All inputs are finite; a program needn't handle non-finite values.
Results may differ from a plain program's by a relative error of at most 0.013.
Values may be sent and summed in bfloat16 or wider, within the bound.
No kernel may reach another device: no remote copies, remote signals or barrier semaphores. Data moves between devices by JAX's collectives and lax.ppermute only.
A program may use at most 64 MiB of HBM per device.

v0:
```python
import jax
import jax.numpy as jnp
from jax import lax
from jax.sharding import PartitionSpec as P

epsilon = 1e-05


def layer_norm(values, norm_gain, reduce_axis):
    average = jnp.mean(values, axis=reduce_axis, keepdims=True)
    centred = values - average
    variance = jnp.mean(centred * centred, axis=reduce_axis, keepdims=True)
    return centred * lax.rsqrt(variance + epsilon) * norm_gain


def project_in(pair_state, norm_gain, project, gate_matrix):
    row_count, col_count, features = pair_state.shape
    flattened = pair_state.reshape(row_count * col_count, features).astype(jnp.float32)
    normed = layer_norm(flattened, norm_gain, 1).astype(jnp.bfloat16)
    projected = jnp.einsum("xc,cd->dx", normed, project, preferred_element_type=jnp.float32)
    left_part = jax.nn.sigmoid(projected[:features]) * projected[features : 2 * features]
    right_part = jax.nn.sigmoid(projected[2 * features : 3 * features]) * projected[3 * features :]
    left_part = left_part.astype(jnp.bfloat16).reshape(features, row_count, col_count)
    right_part = right_part.astype(jnp.bfloat16).reshape(features, row_count, col_count)
    gating = jax.nn.sigmoid(jnp.dot(normed, gate_matrix, preferred_element_type=jnp.float32))
    return (left_part, right_part, gating)


def finish(pair_state, mixture, gating, out_gain, final_matrix):
    features = mixture.shape[0]
    flattened = mixture.reshape(features, -1).astype(jnp.float32)
    normed = layer_norm(flattened, out_gain[:, None], 0).astype(jnp.bfloat16)
    update = jnp.einsum("cx,cd->xd", normed, final_matrix, preferred_element_type=jnp.float32)
    result = pair_state.reshape(-1, features).astype(jnp.float32) + gating * update
    return result.astype(jnp.bfloat16).reshape(pair_state.shape)


def shards(
    pair_input,
    first_gain,
    first_project,
    first_gate,
    first_norm,
    first_final,
    second_gain,
    second_project,
    second_gate,
    second_norm,
    second_final,
):
    left_part, right_part, gating = project_in(pair_input, first_gain, first_project, first_gate)
    left_part, right_part = (
        lax.all_to_all(left_part, ("chan", "sub"), split_axis=0, concat_axis=2, tiled=True),
        lax.all_to_all(right_part, ("chan", "sub"), split_axis=0, concat_axis=2, tiled=True),
    )
    mixture = jnp.einsum(
        "cik,cjk->cij",
        left_part,
        lax.all_gather(right_part, "dap", axis=1, tiled=True),
        preferred_element_type=jnp.float32,
    ).astype(jnp.bfloat16)
    mixture = lax.all_to_all(mixture, ("chan", "sub"), split_axis=2, concat_axis=0, tiled=True)
    middle = finish(pair_input, mixture, gating, first_norm, first_final)
    left_part, right_part, gating = project_in(middle, second_gain, second_project, second_gate)
    left_part, right_part = (
        lax.all_to_all(left_part, ("chan", "sub"), split_axis=0, concat_axis=2, tiled=True),
        lax.all_to_all(right_part, ("chan", "sub"), split_axis=0, concat_axis=2, tiled=True),
    )
    turned = lax.all_to_all(left_part, "dap", split_axis=2, concat_axis=1, tiled=True)
    mixture = jnp.einsum(
        "cki,ckj->cij",
        turned,
        lax.all_gather(right_part, "dap", axis=1, tiled=True),
        preferred_element_type=jnp.float32,
    )
    mixture = lax.all_to_all(
        mixture.astype(jnp.bfloat16), ("chan", "sub"), split_axis=2, concat_axis=0, tiled=True
    )
    return finish(middle, mixture, gating, second_norm, second_final)


def solution(mesh):
    placed = (
        P(("groups", "dap"), ("chan", "sub"), None),
        P(),
        P(),
        P(),
        P(),
        P(),
        P(),
        P(),
        P(),
        P(),
        P(),
    )
    return jax.shard_map(
        shards,
        mesh=mesh,
        in_specs=placed,
        out_specs=P(("groups", "dap"), ("chan", "sub"), None),
        check_vma=False,
    )
```

profile of v0, /device:TPU:0, one launch (start us, length us, event | category | flops | bytes accessed | tf_op | source)
XLA Modules:
  0.0 717.1 jit_solution(18188985698345366559)
XLA Ops:
  31.6 41.2 %all_to_all.108 = bf16[128,96,96]{2,1,0:T(8,128)(2,1)S(1)} all-to-all(bf16[128,96,96]{2,1,0:T(8,128)(2,1)} %copy.28), channel_id=1, replica_groups=mesh['groups'=2,'dap'=4,'chan'=2,'sub'=2] {'chan','sub'}, dimensions={0} | all-to-all | bytes 4718592 | tf_op jit(solution)/shard_map/all_to_all | solution.py:54
  76.9 5.9 all_to_all.86
  87.7 53.0 %all_to_all.109 = bf16[128,96,96]{2,1,0:T(8,128)(2,1)S(1)} all-to-all(bf16[128,96,96]{2,1,0:T(8,128)(2,1)} %copy.26), channel_id=1, replica_groups=mesh['groups'=2,'dap'=4,'chan'=2,'sub'=2] {'chan','sub'}, dimensions={0} | all-to-all | bytes 4718592 | tf_op jit(solution)/shard_map/all_to_all | solution.py:53
  144.7 5.9 all_to_all.82
  150.7 100.2 %all-gather.3.cloned.1.call-done = bf16[32,384,384]{2,1,0:T(8,128)(2,1)} async-done(((bf16[32,96,384]{2,1,0:T(8,128)(2,1)}), bf16[32,384,384]{2,1,0:T(8,128)(2,1)}) %all-gather.3.cloned.1.call-update) | async-done | bytes 9437200 | tf_op jit(solution)/shard_map/all_gather | solution.py:59
  250.9 9.1 %convolution_convert_fusion.1 = bf16[32,96,384]{2,1,0:T(8,128)(2,1)} fusion(bf16[32,96,384]{2,1,0:T(8,128)(2,1)} %all_to_all.82, bf16[32,384,384]{2,1,0:T(8,128)(2,1)} %all-gather.3.cloned.1.call-done), kind=kOutput, calls=%fused_computation.61 | convolution fusion | flops 907149312 | bytes 14155776 | tf_op jit(solution)/shard_map/cik,cjk->cij/dot_general | solution.py:56
  269.7 5.2 fusion.9
  274.9 31.7 %all-to-all-done.2 = bf16[32,96,384]{1,0,2:T(8,128)(2,1)} async-done(((bf16[32,96,384]{1,0,2:T(8,128)(2,1)}), bf16[32,96,384]{1,0,2:T(8,128)(2,1)}, u32[]{:S(2)}, u32[]{:S(2)}) %all-to-all-start.2) | async-done | bytes 2359328 | tf_op jit(solution)/shard_map/all_to_all | solution.py:62
  306.6 6.9 copy.31
  319.2 7.2 %reshape.153 = f32[128,9216]{1,0:T(8,128)} reshape(f32[4,32,96,96]{3,2,1,0:T(8,128)} %bitcast.64) | data formatting | bytes 9437184 | tf_op jit(solution)/shard_map/convert_element_type | solution.py:31
  326.4 5.9 fusion.36
  346.1 40.8 %all_to_all.110 = bf16[128,96,96]{2,1,0:T(8,128)(2,1)S(1)} all-to-all(bf16[128,96,96]{2,1,0:T(8,128)(2,1)} %copy.37), channel_id=1, replica_groups=mesh['groups'=2,'dap'=4,'chan'=2,'sub'=2] {'chan','sub'}, dimensions={0} | all-to-all | bytes 4718592 | tf_op jit(solution)/shard_map/all_to_all | solution.py:67
  390.9 5.9 all_to_all.99
  400.1 42.3 %all_to_all.111 = bf16[128,96,96]{2,1,0:T(8,128)(2,1)} all-to-all(bf16[128,96,96]{2,1,0:T(8,128)(2,1)} %copy.32), channel_id=1, replica_groups=mesh['groups'=2,'dap'=4,'chan'=2,'sub'=2] {'chan','sub'}, dimensions={0} | all-to-all | bytes 4718592 | tf_op jit(solution)/shard_map/all_to_all | solution.py:66
  442.4 6.6 copy.41
  449.0 159.6 %all_to_all.112 = bf16[32,96,384]{1,0,2:T(8,128)(2,1)S(1)} all-to-all(bf16[32,96,384]{1,0,2:T(8,128)(2,1)} %bitcast.71), channel_id=1, replica_groups=mesh['groups'=2,'dap'=4,'chan'=2,'sub'=2] {'dap'}, dimensions={2} | all-to-all | bytes 4718592 | tf_op jit(solution)/shard_map/all_to_all | solution.py:69
  617.6 10.6 %all-gather.5.cloned.1.call-done = bf16[32,384,384]{2,1,0:T(8,128)(2,1)} async-done(((bf16[32,96,384]{2,1,0:T(8,128)(2,1)}), bf16[32,384,384]{2,1,0:T(8,128)(2,1)}) %all-gather.5.cloned.1.call-update) | async-done | bytes 9437200 | tf_op jit(solution)/shard_map/all_gather | solution.py:73
  628.2 7.0 convolution_convert_fusion
  635.2 5.0 copy.39
  645.1 6.7 fusion.10
  651.8 30.3 %all-to-all-done.6 = bf16[32,96,384]{1,0,2:T(8,128)(2,1)} async-done(((bf16[32,96,384]{1,0,2:T(8,128)(2,1)}), bf16[32,96,384]{1,0,2:T(8,128)(2,1)}, u32[]{:S(2)}, u32[]{:S(2)}) %all-to-all-start.6) | async-done | bytes 2359328 | tf_op jit(solution)/shard_map/all_to_all | solution.py:76
  682.1 6.9 copy.40
  694.7 7.2 %reshape.154 = f32[128,9216]{1,0:T(8,128)} reshape(f32[4,32,96,96]{3,2,1,0:T(8,128)} %bitcast.65) | data formatting | bytes 9437184 | tf_op jit(solution)/shard_map/convert_element_type | solution.py:31
  701.9 8.0 %fusion.7 = bf16[9216,128]{1,0:T(8,128)(2,1)} fusion(f32[9216,128]{1,0:T(8,128)} %copy-done.4, f32[9216,128]{1,0:T(8,128)} %fusion.10, bf16[128,128]{1,0:T(8,128)(2,1)S(1)} %copy-done.9, f32[128,9216]{1,0:T(8,128)} %reshape.154, f32[128]{0:T(128)S(1)} %copy-done.13, f32[9216]{0:T(1024)S(1)} %rsqrt.47, f32[9216]{0:T(1024)S(1)} %div.63), kind=kOutput, calls=%fused_computation.13 | convolution fusion | flops 310247424 | bytes 16622080 | tf_op jit(solution)/shard_map/cx,cd->xd/dot_general | solution.py:33
  (74 shorter events, 93.8 us)
Async XLA Ops:
  6.5 13.7 %copy-start = (bf16[128,512]{1,0:T(8,128)(2,1)S(1)}, bf16[128,512]{1,0:T(8,128)(2,1)}, u32[]{:S(2)}) copy-start(bf16[128,512]{1,0:T(8,128)(2,1)} %param.13) | copy-start | bytes 393220
  6.5 7.3 %copy-start.5 = (bf16[96,96,128]{2,1,0:T(8,128)(2,1)S(1)}, bf16[96,96,128]{2,1,0:T(8,128)(2,1)}, u32[]{:S(2)}) copy-start(bf16[96,96,128]{2,1,0:T(8,128)(2,1)} %param.11) | copy-start | bytes 7077892
  6.5 7.3 %copy-start.12 = (f32[128]{0:T(128)S(1)}, f32[128]{0:T(128)}, u32[]{:S(2)}) copy-start(f32[128]{0:T(128)} %param.12) | copy-start | bytes 1540
  6.5 244.4 %all-gather.3.cloned.1.call-start = ((), (), s32[]{:S(2)}) async-start(), calls=%async_computation.7 | async-start | bytes 11796480 | tf_op jit(solution)/shard_map/all_gather | solution.py:59
  18.9 1.4 copy-start.6
  260.0 9.7 %copy-start.14 = (bf16[128,128]{1,0:T(8,128)(2,1)S(1)}, bf16[128,128]{1,0:T(8,128)(2,1)}, u32[]{:S(2)}) copy-start(bf16[128,128]{1,0:T(8,128)(2,1)} %param.14) | copy-start | bytes 98308
  265.0 41.6 %all-to-all-start.2 = ((bf16[32,96,384]{1,0,2:T(8,128)(2,1)}), bf16[32,96,384]{1,0,2:T(8,128)(2,1)}, u32[]{:S(2)}, u32[]{:S(2)}) async-start(bf16[32,96,384]{1,0,2:T(8,128)(2,1)} %copy.30), calls=%async_computation.2 | async-start | bytes 6291456 | tf_op jit(solution)/shard_map/all_to_all | solution.py:62
  269.7 358.5 %all-gather.5.cloned.1.call-start = ((), (), s32[]{:S(2)}) async-start(), calls=%async_computation.8 | async-start | bytes 11796480 | tf_op jit(solution)/shard_map/all_gather | solution.py:73
  313.5 4.6 copy-start.2
  319.2 7.2 %copy-start.8 = (bf16[128,128]{1,0:T(8,128)(2,1)S(1)}, bf16[128,128]{1,0:T(8,128)(2,1)}, u32[]{:S(2)}) copy-start(bf16[128,128]{1,0:T(8,128)(2,1)} %param.16) | copy-start | bytes 98308
  319.2 7.2 %copy-start.11 = (f32[128]{0:T(128)S(1)}, f32[128]{0:T(128)}, u32[]{:S(2)}) copy-start(f32[128]{0:T(128)} %param.15) | copy-start | bytes 1540
  332.3 5.5 copy-start.4
  332.4 2.8 copy-start.7
  332.4 2.8 copy-start.10
  635.2 9.9 %copy-start.15 = (bf16[128,128]{1,0:T(8,128)(2,1)S(1)}, bf16[128,128]{1,0:T(8,128)(2,1)}, u32[]{:S(2)}) copy-start(bf16[128,128]{1,0:T(8,128)(2,1)} %param.19) | copy-start | bytes 98308
  640.2 41.8 %all-to-all-start.6 = ((bf16[32,96,384]{1,0,2:T(8,128)(2,1)}), bf16[32,96,384]{1,0,2:T(8,128)(2,1)}, u32[]{:S(2)}, u32[]{:S(2)}) async-start(bf16[32,96,384]{1,0,2:T(8,128)(2,1)} %copy.39), calls=%async_computation.6 | async-start | bytes 6291456 | tf_op jit(solution)/shard_map/all_to_all | solution.py:76
  689.0 4.6 copy-start.3
  694.6 7.2 %copy-start.9 = (bf16[128,128]{1,0:T(8,128)(2,1)S(1)}, bf16[128,128]{1,0:T(8,128)(2,1)}, u32[]{:S(2)}) copy-start(bf16[128,128]{1,0:T(8,128)(2,1)} %param.21) | copy-start | bytes 98308
  694.7 7.2 %copy-start.13 = (f32[128]{0:T(128)S(1)}, f32[128]{0:T(128)}, u32[]{:S(2)}) copy-start(f32[128]{0:T(128)} %param.20) | copy-start | bytes 1540
  694.7 15.2 %copy-start.1 = (bf16[128,512]{1,0:T(8,128)(2,1)S(1)}, bf16[128,512]{1,0:T(8,128)(2,1)}, u32[]{:S(2)}) copy-start(bf16[128,512]{1,0:T(8,128)(2,1)} %param.13) | copy-start | bytes 393220
Sparse Core Ops, SparseCore 0:
  83.0 167.8 all-gather.2
  397.0 231.1 all-gather.4
where the time goes:
time: 727 us; the launch traced here: 717 us
  blocking collectives  337 us (46%)
  waiting for transfers between devices  173 us (24%)
  local copies, waits for them, and re-layouts  106 us (15%)
  matrix products  47 us (6%)
  other arithmetic  30.8 us (4%)
  between operations  14.1 us (2%)
  starting transfers between devices  9.58 us (1%)
    all_to_all x1, blocking collectives, shards(): lax.all_to_all(left_part, 'dap', split_axis=2, concat_axis=1, tiled=True)  160 us
    all_gather x2, waiting for transfers between devices, shards(): lax.all_gather(right_part, 'dap', axis=1, tiled=True)  111 us
    all_to_all x2, blocking collectives, shards(): lax.all_to_all(left_part, ('chan', 'sub'), split_axis=0, concat_axis=2, t...  95.4 us
    all_to_all x2, blocking collectives, shards(): lax.all_to_all(right_part, ('chan', 'sub'), split_axis=0, concat_axis=2,...  82 us
    all_to_all x1, waiting for transfers between devices, shards(): lax.all_to_all(mixture, ('chan', 'sub'), split_axis=2, concat_axis=0, til...  31.7 us
    all_to_all x1, waiting for transfers between devices, shards(): lax.all_to_all(mixture.astype(jnp.bfloat16), ('chan', 'sub'), split_axis=...  30.3 us
    convert_element_type x4, local copies, waits for them, and re-layouts, finish(): flattened = mixture.reshape(features, -1).astype(jnp.float32)  28.1 us
    all_to_all x4, local copies, waits for them, and re-layouts, shards(): lax.all_to_all(right_part, ('chan', 'sub'), split_axis=0, concat_axis=2,...  20 us
  transfers between devices with their start and end apart: 4, of which 4 were waited for; matrix products, arithmetic and copies ran while one was open for 5% of the time, Pallas kernels for 0%

commit v1 on v0

--- a/solution.py
+++ b/solution.py
@@ -66,7 +66,10 @@
         lax.all_to_all(left_part, ("chan", "sub"), split_axis=0, concat_axis=2, tiled=True),
         lax.all_to_all(right_part, ("chan", "sub"), split_axis=0, concat_axis=2, tiled=True),
     )
-    turned = lax.all_to_all(left_part, "dap", split_axis=2, concat_axis=1, tiled=True)
+    turned = jnp.concatenate(
+        lax.all_to_all(jnp.stack(jnp.split(left_part, lax.axis_size("dap"), axis=2)), "dap", 0, 0),
+        axis=1,
+    )
     mixture = jnp.einsum(
         "cki,ckj->cij",
         turned,

time: 727 us -> 727 us (level)
    reshape x0 -> x2, local copies, waits for them, and re-layouts: none -> 11.4 us  [shards(): jnp.concatenate(lax.all_to_all(jnp.stack(jnp.split(left_part, lax.axis_si...]
    all_to_all x2 -> x0, local copies, waits for them, and re-layouts: 9 us -> none  [shards(): lax.all_to_all(left_part, 'dap', split_axis=2, concat_axis=1, tiled=True)]
    all_to_all x3 -> x4, local copies, waits for them, and re-layouts: 16.5 us -> 19 us  [shards(): lax.all_to_all(left_part, ('chan', 'sub'), split_axis=0, concat_axis=2, t...]
  transfers between devices with their start and end apart: 4 -> 4, of which waited for: 4 -> 4; matrix products, arithmetic and copies ran while one was open for 5% -> 6% of each run, Pallas kernels for 0% -> 0%
where the time goes in v1:
time: 727 us; the launch traced here: 717 us
  blocking collectives  335 us (46%)
  waiting for transfers between devices  168 us (23%)
  local copies, waits for them, and re-layouts  112 us (15%)
  matrix products  47 us (6%)
  other arithmetic  31.7 us (4%)
  between operations  14.1 us (2%)
  starting transfers between devices  9.61 us (1%)
    all_to_all x1, blocking collectives, shards(): lax.all_to_all(jnp.stack(jnp.split(left_part, lax.axis_size('dap'), axis=...  159 us
    all_gather x2, waiting for transfers between devices, shards(): lax.all_gather(right_part, 'dap', axis=1, tiled=True)  106 us
    all_to_all x2, blocking collectives, shards(): lax.all_to_all(left_part, ('chan', 'sub'), split_axis=0, concat_axis=2, t...  93.7 us
    all_to_all x2, blocking collectives, shards(): lax.all_to_all(right_part, ('chan', 'sub'), split_axis=0, concat_axis=2,...  82 us
    all_to_all x1, waiting for transfers between devices, shards(): lax.all_to_all(mixture, ('chan', 'sub'), split_axis=2, concat_axis=0, til...  31.7 us
    all_to_all x1, waiting for transfers between devices, shards(): lax.all_to_all(mixture.astype(jnp.bfloat16), ('chan', 'sub'), split_axis=...  30.3 us
    convert_element_type x4, local copies, waits for them, and re-layouts, finish(): flattened = mixture.reshape(features, -1).astype(jnp.float32)  28.1 us
    all_to_all x4, local copies, waits for them, and re-layouts, shards(): lax.all_to_all(right_part, ('chan', 'sub'), split_axis=0, concat_axis=2,...  20 us
  transfers between devices with their start and end apart: 4, of which 4 were waited for; matrix products, arithmetic and copies ran while one was open for 6% of the time, Pallas kernels for 0%

profile of v1, /device:TPU:0, one launch (start us, length us, event | category | flops | bytes accessed | tf_op | source)
XLA Modules:
  0.0 717.3 jit_solution(16066359954950217453)
XLA Ops:
  31.6 41.2 %all_to_all.95 = bf16[128,96,96]{2,1,0:T(8,128)(2,1)S(1)} all-to-all(bf16[128,96,96]{2,1,0:T(8,128)(2,1)} %copy.42), channel_id=1, replica_groups=mesh['groups'=2,'dap'=4,'chan'=2,'sub'=2] {'chan','sub'}, dimensions={0} | all-to-all | bytes 4718592 | tf_op jit(solution)/shard_map/all_to_all | solution.py:54
  77.0 5.9 all_to_all.76
  87.8 53.0 %all_to_all.96 = bf16[128,96,96]{2,1,0:T(8,128)(2,1)S(1)} all-to-all(bf16[128,96,96]{2,1,0:T(8,128)(2,1)} %copy.40), channel_id=1, replica_groups=mesh['groups'=2,'dap'=4,'chan'=2,'sub'=2] {'chan','sub'}, dimensions={0} | all-to-all | bytes 4718592 | tf_op jit(solution)/shard_map/all_to_all | solution.py:53
  144.8 5.9 all_to_all.72
  150.8 100.2 %all-gather.3.cloned.1.call-done = bf16[32,384,384]{2,1,0:T(8,128)(2,1)} async-done(((bf16[32,96,384]{2,1,0:T(8,128)(2,1)}), bf16[32,384,384]{2,1,0:T(8,128)(2,1)}) %all-gather.3.cloned.1.call-update) | async-done | bytes 9437200 | tf_op jit(solution)/shard_map/all_gather | solution.py:59
  251.0 9.1 %convolution_convert_fusion.1 = bf16[32,96,384]{2,1,0:T(8,128)(2,1)} fusion(bf16[32,96,384]{2,1,0:T(8,128)(2,1)} %all_to_all.72, bf16[32,384,384]{2,1,0:T(8,128)(2,1)} %all-gather.3.cloned.1.call-done), kind=kOutput, calls=%fused_computation.61 | convolution fusion | flops 907149312 | bytes 14155776 | tf_op jit(solution)/shard_map/cik,cjk->cij/dot_general | solution.py:56
  269.8 5.2 fusion.9
  275.0 31.7 %all-to-all-done.2 = bf16[32,96,384]{1,0,2:T(8,128)(2,1)} async-done(((bf16[32,96,384]{1,0,2:T(8,128)(2,1)}), bf16[32,96,384]{1,0,2:T(8,128)(2,1)}, u32[]{:S(2)}, u32[]{:S(2)}) %all-to-all-start.2) | async-done | bytes 2359328 | tf_op jit(solution)/shard_map/all_to_all | solution.py:62
  306.7 6.9 copy.45
  319.3 7.2 %reshape.161 = f32[128,9216]{1,0:T(8,128)} reshape(f32[4,32,96,96]{3,2,1,0:T(8,128)} %bitcast.67) | data formatting | bytes 9437184 | tf_op jit(solution)/shard_map/convert_element_type | solution.py:31
  326.5 5.9 fusion.36
  346.3 40.8 %all_to_all.97 = bf16[128,96,96]{2,1,0:T(8,128)(2,1)S(1)} all-to-all(bf16[128,96,96]{2,1,0:T(8,128)(2,1)} %copy.49), channel_id=1, replica_groups=mesh['groups'=2,'dap'=4,'chan'=2,'sub'=2] {'chan','sub'}, dimensions={0} | all-to-all | bytes 4718592 | tf_op jit(solution)/shard_map/all_to_all | solution.py:67
  391.1 5.9 all_to_all.86
  400.2 40.7 %all_to_all.98 = bf16[128,96,96]{2,1,0:T(8,128)(2,1)S(1)} all-to-all(bf16[128,96,96]{2,1,0:T(8,128)(2,1)} %copy.46), channel_id=1, replica_groups=mesh['groups'=2,'dap'=4,'chan'=2,'sub'=2] {'chan','sub'}, dimensions={0} | all-to-all | bytes 4718592 | tf_op jit(solution)/shard_map/all_to_all | solution.py:66
  451.7 159.2 %all_to_all.99 = bf16[4,32,96,96]{3,2,1,0:T(8,128)(2,1)} all-to-all(bf16[4,32,96,96]{3,2,1,0:T(8,128)(2,1)S(1)} %pad_maximum_fusion), channel_id=1, replica_groups=mesh['groups'=2,'dap'=4,'chan'=2,'sub'=2] {'dap'}, dimensions={0} | all-to-all | bytes 4718592 | tf_op jit(solution)/shard_map/all_to_all | solution.py:70
  610.9 6.5 copy.48
  622.3 6.0 all-gather.5.cloned.1.call-done
  628.4 7.0 convolution_convert_fusion
  635.4 5.0 copy.51
  645.3 6.7 fusion.10
  652.0 30.3 %all-to-all-done.6 = bf16[32,96,384]{1,0,2:T(8,128)(2,1)} async-done(((bf16[32,96,384]{1,0,2:T(8,128)(2,1)}), bf16[32,96,384]{1,0,2:T(8,128)(2,1)}, u32[]{:S(2)}, u32[]{:S(2)}) %all-to-all-start.6) | async-done | bytes 2359328 | tf_op jit(solution)/shard_map/all_to_all | solution.py:79
  682.3 6.9 copy.52
  694.9 7.2 %reshape.162 = f32[128,9216]{1,0:T(8,128)} reshape(f32[4,32,96,96]{3,2,1,0:T(8,128)} %bitcast.68) | data formatting | bytes 9437184 | tf_op jit(solution)/shard_map/convert_element_type | solution.py:31
  702.0 8.0 %fusion.7 = bf16[9216,128]{1,0:T(8,128)(2,1)} fusion(f32[9216,128]{1,0:T(8,128)} %copy-done.4, f32[9216,128]{1,0:T(8,128)} %fusion.10, bf16[128,128]{1,0:T(8,128)(2,1)S(1)} %copy-done.9, f32[128,9216]{1,0:T(8,128)} %reshape.162, f32[128]{0:T(128)S(1)} %copy-done.13, f32[9216]{0:T(1024)S(1)} %rsqrt.47, f32[9216]{0:T(1024)S(1)} %div.63), kind=kOutput, calls=%fused_computation.13 | convolution fusion | flops 310247424 | bytes 16622080 | tf_op jit(solution)/shard_map/cx,cd->xd/dot_general | solution.py:33
  (77 shorter events, 100.7 us)
Async XLA Ops:
  6.5 13.7 %copy-start = (bf16[128,512]{1,0:T(8,128)(2,1)S(1)}, bf16[128,512]{1,0:T(8,128)(2,1)}, u32[]{:S(2)}) copy-start(bf16[128,512]{1,0:T(8,128)(2,1)} %param.13) | copy-start | bytes 393220
  6.5 7.3 %copy-start.5 = (bf16[96,96,128]{2,1,0:T(8,128)(2,1)S(1)}, bf16[96,96,128]{2,1,0:T(8,128)(2,1)}, u32[]{:S(2)}) copy-start(bf16[96,96,128]{2,1,0:T(8,128)(2,1)} %param.11) | copy-start | bytes 7077892
  6.5 7.3 %copy-start.12 = (f32[128]{0:T(128)S(1)}, f32[128]{0:T(128)}, u32[]{:S(2)}) copy-start(f32[128]{0:T(128)} %param.12) | copy-start | bytes 1540
  6.5 244.4 %all-gather.3.cloned.1.call-start = ((), (), s32[]{:S(2)}) async-start(), calls=%async_computation.7 | async-start | bytes 11796480 | tf_op jit(solution)/shard_map/all_gather | solution.py:59
  18.9 1.4 copy-start.6
  260.0 9.8 %copy-start.14 = (bf16[128,128]{1,0:T(8,128)(2,1)S(1)}, bf16[128,128]{1,0:T(8,128)(2,1)}, u32[]{:S(2)}) copy-start(bf16[128,128]{1,0:T(8,128)(2,1)} %param.14) | copy-start | bytes 98308
  265.1 41.6 %all-to-all-start.2 = ((bf16[32,96,384]{1,0,2:T(8,128)(2,1)}), bf16[32,96,384]{1,0,2:T(8,128)(2,1)}, u32[]{:S(2)}, u32[]{:S(2)}) async-start(bf16[32,96,384]{1,0,2:T(8,128)(2,1)} %copy.44), calls=%async_computation.2 | async-start | bytes 6291456 | tf_op jit(solution)/shard_map/all_to_all | solution.py:62
  269.7 358.6 %all-gather.5.cloned.1.call-start = ((), (), s32[]{:S(2)}) async-start(), calls=%async_computation.8 | async-start | bytes 11796480 | tf_op jit(solution)/shard_map/all_gather | solution.py:76
  313.6 4.6 copy-start.2
  319.3 7.2 %copy-start.8 = (bf16[128,128]{1,0:T(8,128)(2,1)S(1)}, bf16[128,128]{1,0:T(8,128)(2,1)}, u32[]{:S(2)}) copy-start(bf16[128,128]{1,0:T(8,128)(2,1)} %param.16) | copy-start | bytes 98308
  319.3 7.2 %copy-start.11 = (f32[128]{0:T(128)S(1)}, f32[128]{0:T(128)}, u32[]{:S(2)}) copy-start(f32[128]{0:T(128)} %param.15) | copy-start | bytes 1540
  332.4 5.5 copy-start.4
  332.4 2.8 copy-start.7
  332.4 2.8 copy-start.10
  635.4 10.0 %copy-start.15 = (bf16[128,128]{1,0:T(8,128)(2,1)S(1)}, bf16[128,128]{1,0:T(8,128)(2,1)}, u32[]{:S(2)}) copy-start(bf16[128,128]{1,0:T(8,128)(2,1)} %param.19) | copy-start | bytes 98308
  640.4 41.9 %all-to-all-start.6 = ((bf16[32,96,384]{1,0,2:T(8,128)(2,1)}), bf16[32,96,384]{1,0,2:T(8,128)(2,1)}, u32[]{:S(2)}, u32[]{:S(2)}) async-start(bf16[32,96,384]{1,0,2:T(8,128)(2,1)} %copy.51), calls=%async_computation.6 | async-start | bytes 6291456 | tf_op jit(solution)/shard_map/all_to_all | solution.py:79
  689.1 4.6 copy-start.3
  694.8 7.2 %copy-start.9 = (bf16[128,128]{1,0:T(8,128)(2,1)S(1)}, bf16[128,128]{1,0:T(8,128)(2,1)}, u32[]{:S(2)}) copy-start(bf16[128,128]{1,0:T(8,128)(2,1)} %param.21) | copy-start | bytes 98308
  694.8 7.2 %copy-start.13 = (f32[128]{0:T(128)S(1)}, f32[128]{0:T(128)}, u32[]{:S(2)}) copy-start(f32[128]{0:T(128)} %param.20) | copy-start | bytes 1540
  694.8 15.2 %copy-start.1 = (bf16[128,512]{1,0:T(8,128)(2,1)S(1)}, bf16[128,512]{1,0:T(8,128)(2,1)}, u32[]{:S(2)}) copy-start(bf16[128,512]{1,0:T(8,128)(2,1)} %param.13) | copy-start | bytes 393220
Sparse Core Ops, SparseCore 0:
  83.0 167.8 all-gather.2
  397.2 231.1 all-gather.4
